TPU v7x, 32 devices: a whole 2x2x4 slice. The times are simulated.
32 devices in a mesh: rows: 8 (over z, x), cols: 4 (over y, core).
Axes of the slice: x: 2, y: 2, z: 4, core: 2. Of those that a mesh axis runs over, the one named last changes fastest.
Arguments:
- query: bfloat16 [24, 256, 2048], P('rows', 'cols'), may hold values from -6 to 6
- key: bfloat16 [24, 256, 2048], P('rows', 'cols'), may hold values from -6 to 6
- value: bfloat16 [24, 256, 2048], P('rows', 'cols'), may hold values from -6 to 6
- cotangent: bfloat16 [24, 256, 2048], P('rows', 'cols'), may hold values from -6 to 6
- conv_weight: bfloat16 [9, 2048], replicated, may hold values from -1.1953125 to 1.1953125
- row_mask: int32 [24, 2, 2], P('rows'), may hold values from 0 to 1, as said below
- col_mask: int32 [256, 3, 3], P('cols'), may hold values from 0 to 1, as said below
Outputs:
- out: bfloat16 [24, 256, 2048], P('rows', 'cols')
- dquery: bfloat16 [24, 256, 2048], P('rows', 'cols')
- dkey: bfloat16 [24, 256, 2048], P('rows', 'cols')
- dvalue: bfloat16 [24, 256, 2048], P('rows', 'cols')
Inputs may be any that keep to these rules, and one draw needn't show every extreme that they name: `row_mask`: every diagonal block is 1: a query block always sees its own block. `col_mask`: every diagonal block is 1: a query block always sees its own block.
All inputs are finite; a program needn't handle non-finite values.
Results may differ from a plain program's by a relative error of at most 0.011.
Values may be sent and summed in bfloat16 or wider, within the bound.
A program may use at most 128 MiB of HBM per device.

v0:
```python
import math
import jax
import jax.numpy as jnp
from jax import lax
from jax.sharding import PartitionSpec as P

HEAD_DIM = 128
SHEET_ROW_BLOCKS = 2
COL_BLOCKS = 3


def padded(array, sides, width):
    for axis, dim in sides:
        devices, length = (lax.axis_size(axis), array.shape[dim])
        up = [(i, (i + 1) % devices) for i in range(devices - 1)]
        down = [(j, i) for i, j in up]
        last = lax.slice_in_dim(array, length - width, length, axis=dim)
        leading = lax.slice_in_dim(array, 0, width, axis=dim)
        before = lax.ppermute(last, axis, up)
        after = lax.ppermute(leading, axis, down)
        array = jnp.concatenate([before, array, after], axis=dim)
    return array


def block_allow(block_mask_table, query_pos, key_pos, block_len, block_count):
    labels = jnp.arange(block_count)
    query_onehot_rows = (query_pos[:, None] // block_len == labels[None, :]).astype(jnp.float32)
    key_onehot_rows = (key_pos[:, None] // block_len == labels[None, :]).astype(jnp.float32)
    merged_links = jnp.einsum(
        "xv,zvs,hs->zxh", query_onehot_rows, block_mask_table.astype(jnp.float32), key_onehot_rows
    )
    return merged_links > 0.5


def line_attention(query_part, key_part, value_part, grad_part, allowed, layout):
    if layout == "bq":
        query_form = "bqhd"
        key_layout_shape = "bkhd"
    else:
        query_form = "qbhd"
        key_layout_shape = "kbhd"
    score_scale = 1.0 / math.sqrt(query_part.shape[-1])
    pair_form = query_form + "," + key_layout_shape + "->bhqk"
    scores = (
        jnp.einsum(pair_form, query_part, key_part, preferred_element_type=jnp.float32)
        * score_scale
    )
    scores = jnp.where(allowed[:, None], scores, -jnp.inf)
    highest = jnp.max(scores, axis=-1, keepdims=True)
    weights = jnp.exp(scores - highest)
    weights = weights / jnp.sum(weights, axis=-1, keepdims=True)
    rounded = weights.astype(jnp.bfloat16)
    attended = jnp.einsum(
        "bhqk," + key_layout_shape + "->" + query_form,
        rounded,
        value_part,
        preferred_element_type=jnp.float32,
    )
    dweights = jnp.einsum(pair_form, grad_part, value_part, preferred_element_type=jnp.float32)
    delta = jnp.sum(grad_part.astype(jnp.float32) * attended, axis=-1)
    if layout == "bq":
        delta = jnp.transpose(delta, (0, 2, 1))
    else:
        delta = jnp.transpose(delta, (1, 2, 0))
    dscores = (weights * (dweights - delta[..., None]) * score_scale).astype(jnp.bfloat16)
    dquery = jnp.einsum(
        "bhqk," + key_layout_shape + "->" + query_form,
        dscores,
        key_part,
        preferred_element_type=jnp.float32,
    )
    dkey = jnp.einsum(
        "bhqk," + query_form + "->" + key_layout_shape,
        dscores,
        query_part,
        preferred_element_type=jnp.float32,
    )
    dvalue = jnp.einsum(
        "bhqk," + query_form + "->" + key_layout_shape,
        rounded,
        grad_part,
        preferred_element_type=jnp.float32,
    )
    return (attended, dquery, dkey, dvalue)


def depthwise(padded_field, taps, rows_count, cols_count, reverse_taps):
    summed = jnp.zeros((rows_count, cols_count, taps.shape[1]), jnp.float32)
    for row_offset_start in range(3):
        for offset_col in range(3):
            if reverse_taps:
                start_row = 2 - row_offset_start
                start_col = 2 - offset_col
            else:
                start_row = row_offset_start
                start_col = offset_col
            window = padded_field[
                start_row : start_row + rows_count, start_col : start_col + cols_count
            ]
            summed = summed + taps[row_offset_start * 3 + offset_col] * window.astype(jnp.float32)
    return summed


def body(query, key, value, cotangent, conv_weight, row_mask, col_mask):
    rows_here, cols_here, width = query.shape
    half_width = width // 2
    head_groups = half_width // HEAD_DIM
    row_devices = lax.axis_size("rows")
    col_devices = lax.axis_size("cols")
    sheet_rows = rows_here * row_devices
    sheet_cols = cols_here * col_devices
    taps = conv_weight.astype(jnp.float32)
    padded_value = padded(value, (("rows", 0), ("cols", 1)), 1)
    padded_grad = padded(cotangent, (("rows", 0), ("cols", 1)), 1)
    row_len = sheet_cols // SHEET_ROW_BLOCKS
    keys_row, values_row = (
        lax.all_gather(key[:, :, :half_width], "cols", axis=1, tiled=True),
        lax.all_gather(value[:, :, :half_width], "cols", axis=1, tiled=True),
    )
    col_start = lax.axis_index("cols") * cols_here
    allowed = block_allow(
        row_mask,
        col_start + jnp.arange(cols_here),
        jnp.arange(sheet_cols),
        row_len,
        SHEET_ROW_BLOCKS,
    )
    local_shape = (rows_here, cols_here, head_groups, HEAD_DIM)
    whole_shape = (rows_here, sheet_cols, head_groups, HEAD_DIM)
    results = line_attention(
        query[:, :, :half_width].reshape(local_shape),
        keys_row.reshape(whole_shape),
        values_row.reshape(whole_shape),
        cotangent[:, :, :half_width].reshape(local_shape),
        allowed,
        "bq",
    )
    key_terms = results[2].reshape(rows_here, sheet_cols, half_width)
    value_terms = results[3].reshape(rows_here, sheet_cols, half_width)
    key_grads, value_grads = (
        lax.psum_scatter(key_terms, "cols", scatter_dimension=1, tiled=True),
        lax.psum_scatter(value_terms, "cols", scatter_dimension=1, tiled=True),
    )
    out_row = results[0].reshape(rows_here, cols_here, half_width).astype(jnp.bfloat16)
    dq_row = results[1].reshape(rows_here, cols_here, half_width).astype(jnp.bfloat16)
    dk_row = key_grads.astype(jnp.bfloat16)
    dv_row = value_grads.astype(jnp.bfloat16)
    columns_each = cols_here // row_devices
    moved = (
        lax.all_to_all(query[:, :, half_width:], "rows", split_axis=1, concat_axis=0, tiled=True),
        lax.all_to_all(key[:, :, half_width:], "rows", split_axis=1, concat_axis=0, tiled=True),
        lax.all_to_all(value[:, :, half_width:], "rows", split_axis=1, concat_axis=0, tiled=True),
        lax.all_to_all(
            cotangent[:, :, half_width:], "rows", split_axis=1, concat_axis=0, tiled=True
        ),
    )
    column_shape = (sheet_rows, columns_each, head_groups, HEAD_DIM)
    my_tables = lax.dynamic_slice_in_dim(
        col_mask, lax.axis_index("rows") * columns_each, columns_each, 0
    )
    col_len = sheet_rows // COL_BLOCKS
    positions = jnp.arange(sheet_rows)
    col_allowed = block_allow(my_tables, positions, positions, col_len, COL_BLOCKS)
    col_results = line_attention(
        moved[0].reshape(column_shape),
        moved[1].reshape(column_shape),
        moved[2].reshape(column_shape),
        moved[3].reshape(column_shape),
        col_allowed,
        "qb",
    )
    column_flat = (sheet_rows, columns_each, half_width)
    col_pieces = [piece.reshape(column_flat).astype(jnp.bfloat16) for piece in col_results]
    out_col, dq_col, dk_col, dv_col = (
        lax.all_to_all(col_pieces[0], "rows", split_axis=0, concat_axis=1, tiled=True),
        lax.all_to_all(col_pieces[1], "rows", split_axis=0, concat_axis=1, tiled=True),
        lax.all_to_all(col_pieces[2], "rows", split_axis=0, concat_axis=1, tiled=True),
        lax.all_to_all(col_pieces[3], "rows", split_axis=0, concat_axis=1, tiled=True),
    )
    lepe = depthwise(padded_value, taps, rows_here, cols_here, False)
    back_conv = depthwise(padded_grad, taps, rows_here, cols_here, True)
    attended16 = jnp.concatenate([out_row, out_col], axis=2)
    out = (attended16.astype(jnp.float32) + lepe).astype(jnp.bfloat16)
    dquery = jnp.concatenate([dq_row, dq_col], axis=2)
    dkey = jnp.concatenate([dk_row, dk_col], axis=2)
    dvalue_attn = jnp.concatenate([dv_row, dv_col], axis=2)
    dvalue = (dvalue_attn.astype(jnp.float32) + back_conv).astype(jnp.bfloat16)
    return (out, dquery, dkey, dvalue)


def solution(mesh):
    return jax.shard_map(
        body,
        mesh=mesh,
        in_specs=(
            P("rows", "cols", None),
            P("rows", "cols", None),
            P("rows", "cols", None),
            P("rows", "cols", None),
            P(),
            P("rows", None, None),
            P("cols", None, None),
        ),
        out_specs=(
            P("rows", "cols", None),
            P("rows", "cols", None),
            P("rows", "cols", None),
            P("rows", "cols", None),
        ),
        check_vma=False,
    )
```

profile of v0, /device:TPU:1, one launch (start us, length us, event | category | flops | bytes accessed | tf_op | source)
XLA Modules:
  0.0 257.9 jit_solution(13641217916702605888)
XLA Ops:
  13.5 18.9 %all-gather.3.cloned.1.call-done = bf16[3,256,1024]{2,1,0:T(8,128)(2,1)} async-done(((bf16[3,64,1024]{2,1,0:T(8,128)(2,1)}), bf16[3,256,1024]{2,1,0:T(8,128)(2,1)}) %all-gather.3.cloned.1.call-update) | async-done | bytes 1572880 | tf_op jit(solution)/shard_map/all_gather | solution.py:117
  38.5 15.7 %all-gather.5.cloned.1.call-done = bf16[3,256,1024]{2,1,0:T(8,128)(2,1)} async-done(((bf16[3,64,1024]{2,1,0:T(8,128)(2,1)}), bf16[3,256,1024]{2,1,0:T(8,128)(2,1)}) %all-gather.5.cloned.1.call-update) | async-done | bytes 1572880 | tf_op jit(solution)/shard_map/all_gather | solution.py:118
  56.7 6.6 %multiply_reduce_fusion.1 = (f32[3,64,8]{1,2,0:T(8,128)}, bf16[3,8,8,8,128]{4,3,2,1,0:T(8,128)(2,1)}) fusion(bf16[3,8,8,8,128]{4,3,2,1,0:T(8,128)(2,1)} %get-tuple-element.12, bf16[3,256,8,128]{1,3,2,0:T(8,128)(2,1)} %bitcast.155, f32[3,8,64]{2,1,0:T(8,128)} %get-tuple-element.36, f32[3,8,64,256]{3,2,1,0:T(8,128)} %copy-done.3), kind=kOutput, calls=%fused_computation.64 | convolution fusion | flops 102629632 | bytes 3944448 | tf_op jit(solution)/shard_map/bhqk,bkhd->bqhd/dot_general | solution.py:53
  68.2 3.5 %copy.137 = f32[3,256,1024]{2,1,0:T(8,128)} copy(f32[3,256,1024]{1,2,0:T(8,128)} %bitcast.153) | data formatting | bytes 6291456 | tf_op jit(solution)/shard_map/reshape | solution.py:138
  74.0 5.2 %all-to-all-start = ((bf16[3,64,1024]{2,0,1:T(4,128)(2,1)}), bf16[3,64,1024]{2,0,1:T(4,128)(2,1)}, u32[]{:S(2)}, u32[]{:S(2)}) async-start(bf16[3,64,1024]{2,0,1:T(4,128)(2,1)} %copy.154), calls=%async_computation | async-start | bytes 1048576 | tf_op jit(solution)/shard_map/all_to_all | solution.py:150
  80.4 12.7 %all-to-all-done = bf16[3,64,1024]{2,0,1:T(4,128)(2,1)} async-done(((bf16[3,64,1024]{2,0,1:T(4,128)(2,1)}), bf16[3,64,1024]{2,0,1:T(4,128)(2,1)}, u32[]{:S(2)}, u32[]{:S(2)}) %all-to-all-start) | async-done | bytes 393248 | tf_op jit(solution)/shard_map/all_to_all | solution.py:150
  93.1 4.6 %all-to-all-start.1 = ((bf16[3,64,1024]{2,0,1:T(4,128)(2,1)}), bf16[3,64,1024]{2,0,1:T(4,128)(2,1)}, u32[]{:S(2)}, u32[]{:S(2)}) async-start(bf16[3,64,1024]{2,0,1:T(4,128)(2,1)} %copy.155), calls=%async_computation.1 | async-start | bytes 1048576 | tf_op jit(solution)/shard_map/all_to_all | solution.py:151
  99.7 4.7 %collective-permute-start = (bf16[1,64,2048]{2,1,0:T(8,128)(2,1)}, bf16[1,64,2048]{2,1,0:T(8,128)(2,1)}, u32[]{:S(2)}, u32[]{:S(2)}) collective-permute-start(bf16[1,64,2048]{2,1,0:T(8,128)(2,1)} %get-tuple-element.23), channel_id=1, source_target_pairs={{0,4},{4,8},{8,12},{12,16},{16,20},{20,24},{24,28},{1,5},{5,9},{9,... | collective-permute-start | bytes 786440 | tf_op jit(solution)/shard_map/ppermute | solution.py:19
  106.6 3.0 %all-to-all-done.1 = bf16[3,64,1024]{2,0,1:T(4,128)(2,1)} async-done(((bf16[3,64,1024]{2,0,1:T(4,128)(2,1)}), bf16[3,64,1024]{2,0,1:T(4,128)(2,1)}, u32[]{:S(2)}, u32[]{:S(2)}) %all-to-all-start.1) | async-done | bytes 393248 | tf_op jit(solution)/shard_map/all_to_all | solution.py:151
  109.6 6.3 %all-to-all-start.2 = ((bf16[3,64,1024]{2,0,1:T(4,128)(2,1)}), bf16[3,64,1024]{2,0,1:T(4,128)(2,1)}, u32[]{:S(2)}, u32[]{:S(2)}) async-start(bf16[3,64,1024]{2,0,1:T(4,128)(2,1)} %copy.156), calls=%async_computation.2 | async-start | bytes 1048576 | tf_op jit(solution)/shard_map/all_to_all | solution.py:152
  118.0 4.7 %collective-permute-start.4 = (bf16[1,64,2048]{2,1,0:T(8,128)(2,1)}, bf16[1,64,2048]{2,1,0:T(8,128)(2,1)}, u32[]{:S(2)}, u32[]{:S(2)}) collective-permute-start(bf16[1,64,2048]{2,1,0:T(8,128)(2,1)} %get-tuple-element.9), channel_id=1, source_target_pairs={{0,4},{4,8},{8,12},{12,16},{16,20},{20,24},{24,28},{1,5},{5,9},{9,... | collective-permute-start | bytes 786440 | tf_op jit(solution)/shard_map/ppermute | solution.py:19
  126.4 6.6 %all-to-all-start.4 = ((bf16[3,64,1024]{2,0,1:T(4,128)(2,1)}), bf16[3,64,1024]{2,0,1:T(4,128)(2,1)}, u32[]{:S(2)}, u32[]{:S(2)}) async-start(bf16[3,64,1024]{2,0,1:T(4,128)(2,1)} %copy.157), calls=%async_computation.4 | async-start | bytes 1048576 | tf_op jit(solution)/shard_map/all_to_all | solution.py:153
  133.3 6.8 %fusion.23 = f32[3,8,256,128]{2,3,1,0:T(8,128)} fusion(bf16[3,8,8,8,128]{4,3,2,1,0:T(8,128)(2,1)} %get-tuple-element.12, f32[3,8,64]{2,1,0:T(8,128)} %get-tuple-element.36, f32[3,8,64,256]{3,2,1,0:T(8,128)} %copy-done.3), kind=kOutput, calls=%fused_computation.73 | convolution fusion | flops 101844736 | bytes 5117952 | tf_op jit(solution)/shard_map/bhqk,bqhd->bkhd/dot_general | solution.py:78
  140.0 3.6 %copy.142 = f32[3,256,1024]{2,1,0:T(8,128)} copy(f32[3,256,1024]{1,2,0:T(8,128)} %bitcast.154) | data formatting | bytes 6291456 | tf_op jit(solution)/shard_map/reshape | solution.py:139
  156.2 3.3 %fusion.12 = bf16[24,8,8,128]{3,0,2,1:T(8,128)(2,1)} fusion(bf16[24,8,8,128]{3,2,1,0:T(8,128)(2,1)} %get-tuple-element.40, f32[8,8,24]{2,1,0:T(8,128)} %get-tuple-element.33, f32[8,8,24,24]{2,3,1,0:T(8,128)} %copy-done.17), kind=kOutput, calls=%fused_computation.40 | convolution fusion | flops 9745943 | bytes 940032 | tf_op jit(solution)/shard_map/bhqk,qbhd->kbhd/dot_general | solution.py:78
  161.5 5.3 %all-to-all-start.7 = ((bf16[24,8,1024]{2,1,0:T(8,128)(2,1)}), bf16[24,8,1024]{2,1,0:T(8,128)(2,1)S(1)}, u32[]{:S(2)}, u32[]{:S(2)}) async-start(bf16[24,8,1024]{2,1,0:T(8,128)(2,1)} %convert_element_type.188), calls=%async_computation.9 | async-start | bytes 786432 | tf_op jit(solution)/shard_map/all_to_all | solution.py:178
  166.8 3.7 %multiply_reduce_fusion = (f32[24,8,8]{0,2,1:T(8,128)}, bf16[24,8,8,128]{3,0,2,1:T(8,128)(2,1)}) fusion(bf16[24,8,8,128]{3,2,1,0:T(8,128)(2,1)} %get-tuple-element.40, bf16[24,8,8,128]{3,2,1,0:T(8,128)(2,1)} %get-tuple-element.41, f32[8,8,24]{2,1,0:T(8,128)} %get-tuple-element.33, f32[8,8,24,24]{2,3,1,0:T(8,128)} %copy-done.17), kind=kOutput, calls=%fused_computation.63 | convolution fusion | flops 10334231 | bytes 1339392 | tf_op jit(solution)/shard_map/bhqk,kbhd->qbhd/dot_general | solution.py:53
  176.1 5.5 %all-to-all-start.6 = ((bf16[24,8,1024]{2,1,0:T(8,128)(2,1)}), bf16[24,8,1024]{2,1,0:T(8,128)(2,1)}, u32[]{:S(2)}, u32[]{:S(2)}) async-start(bf16[24,8,1024]{2,1,0:T(8,128)(2,1)} %convert_element_type.184), calls=%async_computation.7 | async-start | bytes 786432 | tf_op jit(solution)/shard_map/all_to_all | solution.py:177
  189.7 4.1 %all-to-all-start.5 = ((bf16[24,8,1024]{2,1,0:T(8,128)(2,1)}), bf16[24,8,1024]{2,1,0:T(8,128)(2,1)}, u32[]{:S(2)}, u32[]{:S(2)}) async-start(bf16[24,8,1024]{2,1,0:T(8,128)(2,1)} %convert_element_type.180), calls=%async_computation.5 | async-start | bytes 786432 | tf_op jit(solution)/shard_map/all_to_all | solution.py:176
  197.2 8.9 %collective-permute-start.6 = (bf16[5,1,2048]{2,1,0:T(2,128)(2,1)}, bf16[5,1,2048]{2,1,0:T(2,128)(2,1)}, u32[]{:S(2)}, u32[]{:S(2)}) collective-permute-start(bf16[5,1,2048]{2,1,0:T(2,128)(2,1)} %get-tuple-element.4), channel_id=1, source_target_pairs={{1,0},{2,1},{3,2},{5,4},{6,5},{7,6},{9,8},{10,9},{11,10},{13,12},{... | collective-permute-start | bytes 61448 | tf_op jit(solution)/shard_map/ppermute | solution.py:20
  213.5 5.6 %all-to-all-start.3 = ((bf16[24,8,1024]{2,1,0:T(8,128)(2,1)}), bf16[24,8,1024]{2,1,0:T(8,128)(2,1)}, u32[]{:S(2)}, u32[]{:S(2)}) async-start(bf16[24,8,1024]{2,1,0:T(8,128)(2,1)} %convert_element_type.158), calls=%async_computation.3 | async-start | bytes 786432 | tf_op jit(solution)/shard_map/all_to_all | solution.py:175
  223.5 3.3 %collective-permute-start.2 = (bf16[5,1,2048]{2,1,0:T(2,128)(2,1)}, bf16[5,1,2048]{2,1,0:T(2,128)(2,1)}, u32[]{:S(2)}, u32[]{:S(2)}) collective-permute-start(bf16[5,1,2048]{2,1,0:T(2,128)(2,1)} %get-tuple-element.6), channel_id=1, source_target_pairs={{0,1},{1,2},{2,3},{4,5},{5,6},{6,7},{8,9},{9,10},{10,11},{12,13},{... | collective-permute-start | bytes 61448 | tf_op jit(solution)/shard_map/ppermute | solution.py:19
  237.2 4.8 %add_convert_fusion.1 = bf16[3,64,2048]{2,1,0:T(8,128)(2,1)} fusion(bf16[3,64,2048]{2,1,0:T(8,128)(2,1)S(1)} %copy-done.1, bf16[5,64,2048]{2,1,0:T(8,128)(2,1)S(1)} %copy-done.5, bf16[5,1,2048]{2,1,0:T(2,128)(2,1)} %collective-permute-done.3, bf16[5,1,2048]{2,1,0:T(2,128)(2,1)} %collective-permute-done.2, bf16[1,64,2048]{2,1,0:T(8,128)(2,1)} %collective-permute-done.1, ...), kind=kLoop, calls=%fused_computation.13 | loop fusion | flops 22020096 | bytes 4308992 | tf_op jit(solution)/shard_map/convert_element_type | solution.py:183
  245.3 6.1 %add_convert_fusion = bf16[3,64,2048]{2,1,0:T(8,128)(2,1)} fusion(bf16[3,64,2048]{2,1,0:T(8,128)(2,1)S(1)} %copy-done.2, bf16[5,64,2048]{2,1,0:T(8,128)(2,1)} %constant_dynamic-update-slice_fusion.3, bf16[5,1,2048]{2,1,0:T(2,128)(2,1)} %collective-permute-done.7, bf16[5,1,2048]{2,1,0:T(2,128)(2,1)} %collective-permute-done.6, ...), kind=kLoop, calls=%fused_computation.11 | loop fusion | flops 22020096 | bytes 4308992 | tf_op jit(solution)/shard_map/convert_element_type | solution.py:187
  (153 shorter events, 90.3 us)
Async XLA Ops:
  7.2 115.6 %copy-start = (s32[64,3,3]{0,2,1:T(4,128)S(1)}, s32[64,3,3]{0,2,1:T(4,128)}, u32[]{:S(2)}) copy-start(s32[64,3,3]{0,2,1:T(4,128)} %param.13) | copy-start | bytes 6916
  7.2 25.1 %all-gather.3.cloned.1.call-start = ((), (), s32[]{:S(2)}) async-start(), calls=%async_computation.10 | async-start | bytes 1966080 | tf_op jit(solution)/shard_map/all_gather | solution.py:117
  9.4 3.1 %copy-start.2 = (bf16[3,64,2048]{2,1,0:T(8,128)(2,1)S(1)}, bf16[3,64,2048]{2,1,0:T(8,128)(2,1)}, u32[]{:S(2)}) copy-start(bf16[3,64,2048]{2,1,0:T(8,128)(2,1)} %param.10) | copy-start | bytes 2359300
  9.4 44.7 %all-gather.5.cloned.1.call-start = ((), (), s32[]{:S(2)}) async-start(), calls=%async_computation.11 | async-start | bytes 1966080 | tf_op jit(solution)/shard_map/all_gather | solution.py:118
  10.5 231.5 %reduce-scatter.3.cloned.1.call-start = ((), (), s32[]{:S(2)}) async-start(), calls=%async_computation.12 | async-start | bytes 3932160 | tf_op jit(solution)/shard_map/reduce_scatter | solution.py:141
  71.8 7.4 %copy-start.7 = (bf16[3,64,1024]{2,1,0:T(8,128)(2,1)S(1)}, bf16[3,64,1024]{2,1,0:T(8,128)(2,1)}, u32[]{:S(2)}) copy-start(bf16[3,64,1024]{2,1,0:T(8,128)(2,1)} %get-tuple-element.19) | copy-start | bytes 1179652
  74.0 19.1 %all-to-all-start = ((bf16[3,64,1024]{2,0,1:T(4,128)(2,1)}), bf16[3,64,1024]{2,0,1:T(4,128)(2,1)}, u32[]{:S(2)}, u32[]{:S(2)}) async-start(bf16[3,64,1024]{2,0,1:T(4,128)(2,1)} %copy.154), calls=%async_computation | async-start | bytes 1048576 | tf_op jit(solution)/shard_map/all_to_all | solution.py:150
  93.1 16.5 %all-to-all-start.1 = ((bf16[3,64,1024]{2,0,1:T(4,128)(2,1)}), bf16[3,64,1024]{2,0,1:T(4,128)(2,1)}, u32[]{:S(2)}, u32[]{:S(2)}) async-start(bf16[3,64,1024]{2,0,1:T(4,128)(2,1)} %copy.155), calls=%async_computation.1 | async-start | bytes 1048576 | tf_op jit(solution)/shard_map/all_to_all | solution.py:151
  98.4 121.7 %collective-permute-start.1 = (bf16[1,64,2048]{2,1,0:T(8,128)(2,1)}, bf16[1,64,2048]{2,1,0:T(8,128)(2,1)}, u32[]{:S(2)}, u32[]{:S(2)}) collective-permute-start(bf16[1,64,2048]{2,1,0:T(8,128)(2,1)} %get-tuple-element.22), channel_id=1, source_target_pairs={{4,0},{8,4},{12,8},{16,12},{20,16},{24,20},{28,24},{5,1},{9,5},{13... | collective-permute-start | bytes 786440 | tf_op jit(solution)/shard_map/ppermute | solution.py:20
  99.7 108.4 %collective-permute-start = (bf16[1,64,2048]{2,1,0:T(8,128)(2,1)}, bf16[1,64,2048]{2,1,0:T(8,128)(2,1)}, u32[]{:S(2)}, u32[]{:S(2)}) collective-permute-start(bf16[1,64,2048]{2,1,0:T(8,128)(2,1)} %get-tuple-element.23), channel_id=1, source_target_pairs={{0,4},{4,8},{8,12},{12,16},{16,20},{20,24},{24,28},{1,5},{5,9},{9,... | collective-permute-start | bytes 786440 | tf_op jit(solution)/shard_map/ppermute | solution.py:19
  104.4 20.8 %copy-start.6 = (bf16[3,64,1024]{2,1,0:T(8,128)(2,1)S(1)}, bf16[3,64,1024]{2,1,0:T(8,128)(2,1)}, u32[]{:S(2)}) copy-start(bf16[3,64,1024]{2,1,0:T(8,128)(2,1)} %get-tuple-element.13) | copy-start | bytes 1179652
  109.6 16.8 %all-to-all-start.2 = ((bf16[3,64,1024]{2,0,1:T(4,128)(2,1)}), bf16[3,64,1024]{2,0,1:T(4,128)(2,1)}, u32[]{:S(2)}, u32[]{:S(2)}) async-start(bf16[3,64,1024]{2,0,1:T(4,128)(2,1)} %copy.156), calls=%async_computation.2 | async-start | bytes 1048576 | tf_op jit(solution)/shard_map/all_to_all | solution.py:152
  116.8 77.1 %collective-permute-start.5 = (bf16[1,64,2048]{2,1,0:T(8,128)(2,1)}, bf16[1,64,2048]{2,1,0:T(8,128)(2,1)}, u32[]{:S(2)}, u32[]{:S(2)}) collective-permute-start(bf16[1,64,2048]{2,1,0:T(8,128)(2,1)} %get-tuple-element.8), channel_id=1, source_target_pairs={{4,0},{8,4},{12,8},{16,12},{20,16},{24,20},{28,24},{5,1},{9,5},{13... | collective-permute-start | bytes 786440 | tf_op jit(solution)/shard_map/ppermute | solution.py:20
  118.0 63.6 %collective-permute-start.4 = (bf16[1,64,2048]{2,1,0:T(8,128)(2,1)}, bf16[1,64,2048]{2,1,0:T(8,128)(2,1)}, u32[]{:S(2)}, u32[]{:S(2)}) collective-permute-start(bf16[1,64,2048]{2,1,0:T(8,128)(2,1)} %get-tuple-element.9), channel_id=1, source_target_pairs={{0,4},{4,8},{8,12},{12,16},{16,20},{20,24},{24,28},{1,5},{5,9},{9,... | collective-permute-start | bytes 786440 | tf_op jit(solution)/shard_map/ppermute | solution.py:19
  126.4 23.8 %all-to-all-start.4 = ((bf16[3,64,1024]{2,0,1:T(4,128)(2,1)}), bf16[3,64,1024]{2,0,1:T(4,128)(2,1)}, u32[]{:S(2)}, u32[]{:S(2)}) async-start(bf16[3,64,1024]{2,0,1:T(4,128)(2,1)} %copy.157), calls=%async_computation.4 | async-start | bytes 1048576 | tf_op jit(solution)/shard_map/all_to_all | solution.py:153
  133.0 111.0 %reduce-scatter.5.cloned.1.call-start = ((), (), s32[]{:S(2)}) async-start(), calls=%async_computation.13 | async-start | bytes 3932160 | tf_op jit(solution)/shard_map/reduce_scatter | solution.py:142
  161.5 14.6 %all-to-all-start.7 = ((bf16[24,8,1024]{2,1,0:T(8,128)(2,1)}), bf16[24,8,1024]{2,1,0:T(8,128)(2,1)S(1)}, u32[]{:S(2)}, u32[]{:S(2)}) async-start(bf16[24,8,1024]{2,1,0:T(8,128)(2,1)} %convert_element_type.188), calls=%async_computation.9 | async-start | bytes 786432 | tf_op jit(solution)/shard_map/all_to_all | solution.py:178
  176.1 13.6 %all-to-all-start.6 = ((bf16[24,8,1024]{2,1,0:T(8,128)(2,1)}), bf16[24,8,1024]{2,1,0:T(8,128)(2,1)}, u32[]{:S(2)}, u32[]{:S(2)}) async-start(bf16[24,8,1024]{2,1,0:T(8,128)(2,1)} %convert_element_type.184), calls=%async_computation.7 | async-start | bytes 786432 | tf_op jit(solution)/shard_map/all_to_all | solution.py:177
  189.7 23.8 %all-to-all-start.5 = ((bf16[24,8,1024]{2,1,0:T(8,128)(2,1)}), bf16[24,8,1024]{2,1,0:T(8,128)(2,1)}, u32[]{:S(2)}, u32[]{:S(2)}) async-start(bf16[24,8,1024]{2,1,0:T(8,128)(2,1)} %convert_element_type.180), calls=%async_computation.5 | async-start | bytes 786432 | tf_op jit(solution)/shard_map/all_to_all | solution.py:176
  197.2 48.1 %collective-permute-start.6 = (bf16[5,1,2048]{2,1,0:T(2,128)(2,1)}, bf16[5,1,2048]{2,1,0:T(2,128)(2,1)}, u32[]{:S(2)}, u32[]{:S(2)}) collective-permute-start(bf16[5,1,2048]{2,1,0:T(2,128)(2,1)} %get-tuple-element.4), channel_id=1, source_target_pairs={{1,0},{2,1},{3,2},{5,4},{6,5},{7,6},{9,8},{10,9},{11,10},{13,12},{... | collective-permute-start | bytes 61448 | tf_op jit(solution)/shard_map/ppermute | solution.py:20
  206.1 39.2 %collective-permute-start.7 = (bf16[5,1,2048]{2,1,0:T(2,128)(2,1)}, bf16[5,1,2048]{2,1,0:T(2,128)(2,1)}, u32[]{:S(2)}, u32[]{:S(2)}) collective-permute-start(bf16[5,1,2048]{2,1,0:T(2,128)(2,1)} %get-tuple-element.5), channel_id=1, source_target_pairs={{0,1},{1,2},{2,3},{4,5},{5,6},{6,7},{8,9},{9,10},{10,11},{12,13},{... | collective-permute-start | bytes 61448 | tf_op jit(solution)/shard_map/ppermute | solution.py:19
  213.5 18.9 %all-to-all-start.3 = ((bf16[24,8,1024]{2,1,0:T(8,128)(2,1)}), bf16[24,8,1024]{2,1,0:T(8,128)(2,1)}, u32[]{:S(2)}, u32[]{:S(2)}) async-start(bf16[24,8,1024]{2,1,0:T(8,128)(2,1)} %convert_element_type.158), calls=%async_computation.3 | async-start | bytes 786432 | tf_op jit(solution)/shard_map/all_to_all | solution.py:175
  223.5 13.2 %collective-permute-start.2 = (bf16[5,1,2048]{2,1,0:T(2,128)(2,1)}, bf16[5,1,2048]{2,1,0:T(2,128)(2,1)}, u32[]{:S(2)}, u32[]{:S(2)}) collective-permute-start(bf16[5,1,2048]{2,1,0:T(2,128)(2,1)} %get-tuple-element.6), channel_id=1, source_target_pairs={{0,1},{1,2},{2,3},{4,5},{5,6},{6,7},{8,9},{9,10},{10,11},{12,13},{... | collective-permute-start | bytes 61448 | tf_op jit(solution)/shard_map/ppermute | solution.py:19
  226.8 9.9 %collective-permute-start.3 = (bf16[5,1,2048]{2,1,0:T(2,128)(2,1)}, bf16[5,1,2048]{2,1,0:T(2,128)(2,1)}, u32[]{:S(2)}, u32[]{:S(2)}) collective-permute-start(bf16[5,1,2048]{2,1,0:T(2,128)(2,1)} %get-tuple-element.7), channel_id=1, source_target_pairs={{1,0},{2,1},{3,2},{5,4},{6,5},{7,6},{9,8},{10,9},{11,10},{13,12},{... | collective-permute-start | bytes 61448 | tf_op jit(solution)/shard_map/ppermute | solution.py:20
  (26 other events, 49.4 us)
Sparse Core Ops, SparseCore 0:
  10.2 22.1 all-gather.2
  34.5 19.6 all-gather.4
  71.9 37.5 reduce-scatter.2
  143.8 42.4 reduce-scatter.4
where the time goes:
time: 260 us; the launch traced here: 258 us
  starting transfers between devices  71.8 us (28%)
  local copies, waits for them, and re-layouts  66.4 us (26%)
  waiting for transfers between devices  52.5 us (20%)
  matrix products  33.9 us (13%)
  other arithmetic  18.9 us (7%)
  between operations  14.3 us (6%)
    all_gather x1, waiting for transfers between devices, body(): lax.all_gather(key[:, :, :half_width], 'cols', axis=1, tiled=True)  18.9 us
    unnamed x70, local copies, waits for them, and re-layouts  16.6 us
    all_gather x1, waiting for transfers between devices, body(): lax.all_gather(value[:, :, :half_width], 'cols', axis=1, tiled=True)  15.7 us
    ppermute x4, starting transfers between devices, padded(): before = lax.ppermute(last, axis, up)  14.7 us
    ppermute x4, starting transfers between devices, padded(): after = lax.ppermute(leading, axis, down)  13.6 us
    all_to_all x1, waiting for transfers between devices, body(): lax.all_to_all(query[:, :, half_width:], 'rows', split_axis=1, concat_axi...  12.7 us
    convert_element_type x8, local copies, waits for them, and re-layouts, body(): piece.reshape(column_flat).astype(jnp.bfloat16)  11.3 us
    dot_general x2, matrix products, line_attention(): jnp.einsum('bhqk,' + key_layout_shape + '->' + query_form, rounded, value...  10.4 us
  transfers between devices with their start and end apart: 20, of which 5 were waited for; matrix products, arithmetic and copies ran while one was open for 35% of the time, Pallas kernels for 0%

commit v1 on v0

--- a/solution.py
+++ b/solution.py
@@ -7,6 +7,29 @@
 HEAD_DIM = 128
 SHEET_ROW_BLOCKS = 2
 COL_BLOCKS = 3
+
+
+def split_up(array, dim, count):
+    dims = array.shape
+    pieces = array.reshape(*dims[:dim], count, dims[dim] // count, *dims[dim + 1 :])
+    return jnp.moveaxis(pieces, dim, 0)
+
+
+def joined_along(parts, dim):
+    dims = list(parts.shape[1:])
+    dims[dim] *= parts.shape[0]
+    return jnp.moveaxis(parts, 0, dim).reshape(dims)
+
+
+def exchange_in_pairs(value, axis, split_dim, concat_dim):
+    size, index = (lax.axis_size(axis), lax.axis_index(axis))
+    parts = split_up(value, split_dim, size)
+    outs = [parts[index]]
+    for step in range(1, size):
+        sent = parts[index ^ step]
+        outs.append(lax.ppermute(sent, axis, [(i, i ^ step) for i in range(size)]))
+    parts = jnp.stack(outs)[index ^ jnp.arange(size)]
+    return joined_along(parts, concat_dim)
 
 
 def padded(array, sides, width):
@@ -175,7 +198,7 @@
         lax.all_to_all(col_pieces[0], "rows", split_axis=0, concat_axis=1, tiled=True),
         lax.all_to_all(col_pieces[1], "rows", split_axis=0, concat_axis=1, tiled=True),
         lax.all_to_all(col_pieces[2], "rows", split_axis=0, concat_axis=1, tiled=True),
-        lax.all_to_all(col_pieces[3], "rows", split_axis=0, concat_axis=1, tiled=True),
+        exchange_in_pairs(col_pieces[3], "rows", 0, 1),
     )
     lepe = depthwise(padded_value, taps, rows_here, cols_here, False)
     back_conv = depthwise(padded_grad, taps, rows_here, cols_here, True)

time: 260 us -> 290 us (1.12)
  the two profiles are of different devices: /device:TPU:1 before, /device:TPU:0 now
where the time goes in v1:
time: 290 us; the launch traced here: 287 us
  local copies, waits for them, and re-layouts  77.5 us (27%)
  starting transfers between devices  72.5 us (25%)
  waiting for transfers between devices  66.9 us (23%)
  matrix products  35.1 us (12%)
  other arithmetic  20.9 us (7%)
  between operations  14.4 us (5%)
    unnamed x74, local copies, waits for them, and re-layouts  20.8 us
    all_gather x1, waiting for transfers between devices, body(): lax.all_gather(key[:, :, :half_width], 'cols', axis=1, tiled=True)  19.1 us
    ppermute x7, starting transfers between devices, exchange_in_pairs(): outs.append(lax.ppermute(sent, axis, [(i, i ^ step) for i in range(size)]))  18.9 us
    ppermute x4, starting transfers between devices, padded(): before = lax.ppermute(last, axis, up)  16.3 us
    all_gather x1, waiting for transfers between devices, body(): lax.all_gather(value[:, :, :half_width], 'cols', axis=1, tiled=True)  15.7 us
    ppermute x7, waiting for transfers between devices, exchange_in_pairs(): outs.append(lax.ppermute(sent, axis, [(i, i ^ step) for i in range(size)]))  11.7 us
    convert_element_type x8, local copies, waits for them, and re-layouts, body(): piece.reshape(column_flat).astype(jnp.bfloat16)  11.2 us
    dot_general x2, matrix products, line_attention(): jnp.einsum('bhqk,' + key_layout_shape + '->' + query_form, rounded, value...  10.7 us
  transfers between devices with their start and end apart: 26, of which 10 were waited for; matrix products, arithmetic and copies ran while one was open for 37% of the time, Pallas kernels for 0%

profile of v1, /device:TPU:0, one launch (start us, length us, event | category | flops | bytes accessed | tf_op | source)
XLA Modules:
  0.0 287.3 jit_solution(10318075948981922956)
XLA Ops:
  13.4 19.1 %all-gather.3.cloned.1.call-done = bf16[3,256,1024]{2,1,0:T(8,128)(2,1)} async-done(((bf16[3,64,1024]{2,1,0:T(8,128)(2,1)}), bf16[3,256,1024]{2,1,0:T(8,128)(2,1)}) %all-gather.3.cloned.1.call-update) | async-done | bytes 1572880 | tf_op jit(solution)/shard_map/all_gather | solution.py:140
  38.7 15.7 %all-gather.5.cloned.1.call-done = bf16[3,256,1024]{2,1,0:T(8,128)(2,1)} async-done(((bf16[3,64,1024]{2,1,0:T(8,128)(2,1)}), bf16[3,256,1024]{2,1,0:T(8,128)(2,1)}) %all-gather.5.cloned.1.call-update) | async-done | bytes 1572880 | tf_op jit(solution)/shard_map/all_gather | solution.py:141
  57.0 6.8 %multiply_reduce_fusion.1 = (f32[3,64,8]{1,2,0:T(8,128)}, bf16[3,8,8,8,128]{4,3,2,1,0:T(8,128)(2,1)}) fusion(bf16[3,8,8,8,128]{4,3,2,1,0:T(8,128)(2,1)} %get-tuple-element.12, bf16[3,256,8,128]{1,3,2,0:T(8,128)(2,1)} %bitcast.184, f32[3,8,64]{2,1,0:T(8,128)} %get-tuple-element.44, f32[3,8,64,256]{3,2,1,0:T(8,128)} %copy-done.3), kind=kOutput, calls=%fused_computation.65 | convolution fusion | flops 102629632 | bytes 3944448 | tf_op jit(solution)/shard_map/bhqk,bkhd->bqhd/dot_general | solution.py:76
  68.6 3.5 %copy.136 = f32[3,256,1024]{2,1,0:T(8,128)} copy(f32[3,256,1024]{1,2,0:T(8,128)} %bitcast.182) | data formatting | bytes 6291456 | tf_op jit(solution)/shard_map/reshape | solution.py:161
  74.3 5.4 %collective-permute-start = (bf16[1,64,2048]{2,1,0:T(8,128)(2,1)}, bf16[1,64,2048]{2,1,0:T(8,128)(2,1)}, u32[]{:S(2)}, u32[]{:S(2)}) collective-permute-start(bf16[1,64,2048]{2,1,0:T(8,128)(2,1)} %get-tuple-element.23), channel_id=1, source_target_pairs={{0,4},{4,8},{8,12},{12,16},{16,20},{20,24},{24,28},{1,5},{5,9},{9,... | collective-permute-start | bytes 786440 | tf_op jit(solution)/shard_map/ppermute | solution.py:42
  81.9 5.2 %collective-permute-start.11 = (bf16[1,64,2048]{2,1,0:T(8,128)(2,1)}, bf16[1,64,2048]{2,1,0:T(8,128)(2,1)}, u32[]{:S(2)}, u32[]{:S(2)}) collective-permute-start(bf16[1,64,2048]{2,1,0:T(8,128)(2,1)} %get-tuple-element.9), channel_id=1, source_target_pairs={{0,4},{4,8},{8,12},{12,16},{16,20},{20,24},{24,28},{1,5},{5,9},{9,... | collective-permute-start | bytes 786440 | tf_op jit(solution)/shard_map/ppermute | solution.py:42
  88.3 5.0 %all-to-all-start = ((bf16[3,64,1024]{2,0,1:T(4,128)(2,1)}), bf16[3,64,1024]{2,0,1:T(4,128)(2,1)}, u32[]{:S(2)}, u32[]{:S(2)}) async-start(bf16[3,64,1024]{2,0,1:T(4,128)(2,1)} %copy.153), calls=%async_computation | async-start | bytes 1048576 | tf_op jit(solution)/shard_map/all_to_all | solution.py:173
  102.6 4.7 %all-to-all-done = bf16[3,64,1024]{2,0,1:T(4,128)(2,1)} async-done(((bf16[3,64,1024]{2,0,1:T(4,128)(2,1)}), bf16[3,64,1024]{2,0,1:T(4,128)(2,1)}, u32[]{:S(2)}, u32[]{:S(2)}) %all-to-all-start) | async-done | bytes 393248 | tf_op jit(solution)/shard_map/all_to_all | solution.py:173
  107.2 4.4 %all-to-all-start.1 = ((bf16[3,64,1024]{2,0,1:T(4,128)(2,1)}), bf16[3,64,1024]{2,0,1:T(4,128)(2,1)}, u32[]{:S(2)}, u32[]{:S(2)}) async-start(bf16[3,64,1024]{2,0,1:T(4,128)(2,1)} %copy.154), calls=%async_computation.1 | async-start | bytes 1048576 | tf_op jit(solution)/shard_map/all_to_all | solution.py:174
  116.0 10.4 %all-to-all-done.1 = bf16[3,64,1024]{2,0,1:T(4,128)(2,1)} async-done(((bf16[3,64,1024]{2,0,1:T(4,128)(2,1)}), bf16[3,64,1024]{2,0,1:T(4,128)(2,1)}, u32[]{:S(2)}, u32[]{:S(2)}) %all-to-all-start.1) | async-done | bytes 393248 | tf_op jit(solution)/shard_map/all_to_all | solution.py:174
  126.4 4.1 %all-to-all-start.2 = ((bf16[3,64,1024]{2,0,1:T(4,128)(2,1)}), bf16[3,64,1024]{2,0,1:T(4,128)(2,1)}, u32[]{:S(2)}, u32[]{:S(2)}) async-start(bf16[3,64,1024]{2,0,1:T(4,128)(2,1)} %copy.155), calls=%async_computation.2 | async-start | bytes 1048576 | tf_op jit(solution)/shard_map/all_to_all | solution.py:175
  133.6 3.8 %collective-permute-start.14 = (bf16[5,1,2048]{2,1,0:T(2,128)(2,1)}, bf16[5,1,2048]{2,1,0:T(2,128)(2,1)}, u32[]{:S(2)}, u32[]{:S(2)}) collective-permute-start(bf16[5,1,2048]{2,1,0:T(2,128)(2,1)} %get-tuple-element.5), channel_id=1, source_target_pairs={{0,1},{1,2},{2,3},{4,5},{5,6},{6,7},{8,9},{9,10},{10,11},{12,13},{... | collective-permute-start | bytes 61448 | tf_op jit(solution)/shard_map/ppermute | solution.py:42
  140.0 4.8 %all-to-all-done.2 = bf16[3,64,1024]{2,0,1:T(4,128)(2,1)} async-done(((bf16[3,64,1024]{2,0,1:T(4,128)(2,1)}), bf16[3,64,1024]{2,0,1:T(4,128)(2,1)}, u32[]{:S(2)}, u32[]{:S(2)}) %all-to-all-start.2) | async-done | bytes 393248 | tf_op jit(solution)/shard_map/all_to_all | solution.py:175
  144.9 4.1 %all-to-all-start.4 = ((bf16[3,64,1024]{2,0,1:T(4,128)(2,1)}), bf16[3,64,1024]{2,0,1:T(4,128)(2,1)}, u32[]{:S(2)}, u32[]{:S(2)}) async-start(bf16[3,64,1024]{2,0,1:T(4,128)(2,1)} %copy.156), calls=%async_computation.4 | async-start | bytes 1048576 | tf_op jit(solution)/shard_map/all_to_all | solution.py:176
  149.1 6.7 %fusion.23 = f32[3,8,256,128]{2,3,1,0:T(8,128)} fusion(bf16[3,8,8,8,128]{4,3,2,1,0:T(8,128)(2,1)S(1)} %copy-done.17, f32[3,8,64]{2,1,0:T(8,128)} %get-tuple-element.44, f32[3,8,64,256]{3,2,1,0:T(8,128)} %copy-done.3), kind=kOutput, calls=%fused_computation.74 | convolution fusion | flops 101844736 | bytes 5117952 | tf_op jit(solution)/shard_map/bhqk,bqhd->bkhd/dot_general | solution.py:101
  155.8 3.5 %copy.141 = f32[3,256,1024]{2,1,0:T(8,128)} copy(f32[3,256,1024]{1,2,0:T(8,128)} %bitcast.183) | data formatting | bytes 6291456 | tf_op jit(solution)/shard_map/reshape | solution.py:162
  177.4 3.9 %multiply_reduce_fusion = (f32[24,8,8]{0,2,1:T(8,128)}, bf16[24,8,8,128]{3,0,2,1:T(8,128)(2,1)}) fusion(bf16[24,8,8,128]{3,2,1,0:T(8,128)(2,1)} %get-tuple-element.48, bf16[24,8,8,128]{3,2,1,0:T(8,128)(2,1)} %get-tuple-element.49, f32[8,8,24]{2,1,0:T(8,128)} %get-tuple-element.41, f32[8,8,24,24]{2,3,1,0:T(8,128)} %copy-done.15), kind=kOutput, calls=%fused_computation.64 | convolution fusion | flops 10334231 | bytes 1339392 | tf_op jit(solution)/shard_map/bhqk,kbhd->qbhd/dot_general | solution.py:76
  185.7 5.9 %all-to-all-start.6 = ((bf16[24,8,1024]{2,1,0:T(8,128)(2,1)}), bf16[24,8,1024]{2,1,0:T(8,128)(2,1)S(1)}, u32[]{:S(2)}, u32[]{:S(2)}) async-start(bf16[24,8,1024]{2,1,0:T(8,128)(2,1)} %convert_element_type.185), calls=%async_computation.7 | async-start | bytes 786432 | tf_op jit(solution)/shard_map/all_to_all | solution.py:200
  213.1 4.1 %all-to-all-start.5 = ((bf16[24,8,1024]{2,1,0:T(8,128)(2,1)}), bf16[24,8,1024]{2,1,0:T(8,128)(2,1)}, u32[]{:S(2)}, u32[]{:S(2)}) async-start(bf16[24,8,1024]{2,1,0:T(8,128)(2,1)} %convert_element_type.181), calls=%async_computation.5 | async-start | bytes 786432 | tf_op jit(solution)/shard_map/all_to_all | solution.py:199
  221.4 4.1 %collective-permute-done.6 = bf16[3,8,1024]{2,1,0:T(8,128)(2,1)S(1)} collective-permute-done((bf16[3,8,1024]{2,1,0:T(8,128)(2,1)}, bf16[3,8,1024]{2,1,0:T(8,128)(2,1)S(1)}, u32[]{:S(2)}, u32[]{:S(2)}) %collective-permute-start.6) | collective-permute-done | bytes 49184 | tf_op jit(solution)/shard_map/ppermute | solution.py:30
  225.5 5.0 %collective-permute-start.7 = (bf16[3,8,1024]{2,1,0:T(8,128)(2,1)}, bf16[3,8,1024]{2,1,0:T(8,128)(2,1)S(1)}, u32[]{:S(2)}, u32[]{:S(2)}) collective-permute-start(bf16[3,8,1024]{2,1,0:T(8,128)(2,1)} %get-tuple-element.27), channel_id=1, source_target_pairs={{0,16},{4,20},{8,24},{12,28},{16,0},{20,4},{24,8},{28,12},{1,17},{... | collective-permute-start | bytes 147464 | tf_op jit(solution)/shard_map/ppermute | solution.py:30
  247.5 4.1 %all-to-all-start.3 = ((bf16[24,8,1024]{2,1,0:T(8,128)(2,1)}), bf16[24,8,1024]{2,1,0:T(8,128)(2,1)}, u32[]{:S(2)}, u32[]{:S(2)}) async-start(bf16[24,8,1024]{2,1,0:T(8,128)(2,1)} %convert_element_type.159), calls=%async_computation.3 | async-start | bytes 786432 | tf_op jit(solution)/shard_map/all_to_all | solution.py:198
  265.1 6.2 %add_convert_fusion.1 = bf16[3,64,2048]{2,1,0:T(8,128)(2,1)} fusion(bf16[3,64,2048]{2,1,0:T(8,128)(2,1)S(1)} %copy-done.1, bf16[5,64,2048]{2,1,0:T(8,128)(2,1)} %constant_dynamic-update-slice_fusion, bf16[5,1,2048]{2,1,0:T(2,128)(2,1)} %collective-permute-done.3, bf16[5,1,2048]{2,1,0:T(2,128)(2,1)} %collective-permute-done.2, ...), kind=kLoop, calls=%fused_computation.14 | loop fusion | flops 22020096 | bytes 4308992 | tf_op jit(solution)/shard_map/convert_element_type | solution.py:206
  274.6 6.1 %add_convert_fusion = bf16[3,64,2048]{2,1,0:T(8,128)(2,1)} fusion(bf16[3,64,2048]{2,1,0:T(8,128)(2,1)S(1)} %copy-done.2, bf16[5,64,2048]{2,1,0:T(8,128)(2,1)} %constant_dynamic-update-slice_fusion.3, bf16[5,1,2048]{2,1,0:T(2,128)(2,1)} %collective-permute-done.14, bf16[5,1,2048]{2,1,0:T(2,128)(2,1)} %collective-permute-done.13, ...), kind=kLoop, calls=%fused_computation.12 | loop fusion | flops 22020096 | bytes 4308992 | tf_op jit(solution)/shard_map/convert_element_type | solution.py:210
  (174 shorter events, 126.0 us)
Async XLA Ops:
  7.2 25.4 %all-gather.3.cloned.1.call-start = ((), (), s32[]{:S(2)}) async-start(), calls=%async_computation.9 | async-start | bytes 1966080 | tf_op jit(solution)/shard_map/all_gather | solution.py:140
  9.4 45.0 %all-gather.5.cloned.1.call-start = ((), (), s32[]{:S(2)}) async-start(), calls=%async_computation.10 | async-start | bytes 1966080 | tf_op jit(solution)/shard_map/all_gather | solution.py:141
  10.5 260.8 %reduce-scatter.3.cloned.1.call-start = ((), (), s32[]{:S(2)}) async-start(), calls=%async_computation.11 | async-start | bytes 3932160 | tf_op jit(solution)/shard_map/reduce_scatter | solution.py:164
  73.0 86.3 %collective-permute-start.1 = (bf16[1,64,2048]{2,1,0:T(8,128)(2,1)}, bf16[1,64,2048]{2,1,0:T(8,128)(2,1)}, u32[]{:S(2)}, u32[]{:S(2)}) collective-permute-start(bf16[1,64,2048]{2,1,0:T(8,128)(2,1)} %get-tuple-element.22), channel_id=1, source_target_pairs={{4,0},{8,4},{12,8},{16,12},{20,16},{24,20},{28,24},{5,1},{9,5},{13... | collective-permute-start | bytes 786440 | tf_op jit(solution)/shard_map/ppermute | solution.py:43
  74.3 63.0 %collective-permute-start = (bf16[1,64,2048]{2,1,0:T(8,128)(2,1)}, bf16[1,64,2048]{2,1,0:T(8,128)(2,1)}, u32[]{:S(2)}, u32[]{:S(2)}) collective-permute-start(bf16[1,64,2048]{2,1,0:T(8,128)(2,1)} %get-tuple-element.23), channel_id=1, source_target_pairs={{0,4},{4,8},{8,12},{12,16},{16,20},{20,24},{24,28},{1,5},{5,9},{9,... | collective-permute-start | bytes 786440 | tf_op jit(solution)/shard_map/ppermute | solution.py:42
  80.6 33.7 %collective-permute-start.12 = (bf16[1,64,2048]{2,1,0:T(8,128)(2,1)}, bf16[1,64,2048]{2,1,0:T(8,128)(2,1)}, u32[]{:S(2)}, u32[]{:S(2)}) collective-permute-start(bf16[1,64,2048]{2,1,0:T(8,128)(2,1)} %get-tuple-element.8), channel_id=1, source_target_pairs={{4,0},{8,4},{12,8},{16,12},{20,16},{24,20},{28,24},{5,1},{9,5},{13... | collective-permute-start | bytes 786440 | tf_op jit(solution)/shard_map/ppermute | solution.py:43
  81.9 29.7 %collective-permute-start.11 = (bf16[1,64,2048]{2,1,0:T(8,128)(2,1)}, bf16[1,64,2048]{2,1,0:T(8,128)(2,1)}, u32[]{:S(2)}, u32[]{:S(2)}) collective-permute-start(bf16[1,64,2048]{2,1,0:T(8,128)(2,1)} %get-tuple-element.9), channel_id=1, source_target_pairs={{0,4},{4,8},{8,12},{12,16},{16,20},{20,24},{24,28},{1,5},{5,9},{9,... | collective-permute-start | bytes 786440 | tf_op jit(solution)/shard_map/ppermute | solution.py:42
  88.3 18.9 %all-to-all-start = ((bf16[3,64,1024]{2,0,1:T(4,128)(2,1)}), bf16[3,64,1024]{2,0,1:T(4,128)(2,1)}, u32[]{:S(2)}, u32[]{:S(2)}) async-start(bf16[3,64,1024]{2,0,1:T(4,128)(2,1)} %copy.153), calls=%async_computation | async-start | bytes 1048576 | tf_op jit(solution)/shard_map/all_to_all | solution.py:173
  107.2 19.2 %all-to-all-start.1 = ((bf16[3,64,1024]{2,0,1:T(4,128)(2,1)}), bf16[3,64,1024]{2,0,1:T(4,128)(2,1)}, u32[]{:S(2)}, u32[]{:S(2)}) async-start(bf16[3,64,1024]{2,0,1:T(4,128)(2,1)} %copy.154), calls=%async_computation.1 | async-start | bytes 1048576 | tf_op jit(solution)/shard_map/all_to_all | solution.py:174
  126.4 18.4 %all-to-all-start.2 = ((bf16[3,64,1024]{2,0,1:T(4,128)(2,1)}), bf16[3,64,1024]{2,0,1:T(4,128)(2,1)}, u32[]{:S(2)}, u32[]{:S(2)}) async-start(bf16[3,64,1024]{2,0,1:T(4,128)(2,1)} %copy.155), calls=%async_computation.2 | async-start | bytes 1048576 | tf_op jit(solution)/shard_map/all_to_all | solution.py:175
  132.3 142.4 %collective-permute-start.13 = (bf16[5,1,2048]{2,1,0:T(2,128)(2,1)}, bf16[5,1,2048]{2,1,0:T(2,128)(2,1)}, u32[]{:S(2)}, u32[]{:S(2)}) collective-permute-start(bf16[5,1,2048]{2,1,0:T(2,128)(2,1)} %get-tuple-element.4), channel_id=1, source_target_pairs={{1,0},{2,1},{3,2},{5,4},{6,5},{7,6},{9,8},{10,9},{11,10},{13,12},{... | collective-permute-start | bytes 61448 | tf_op jit(solution)/shard_map/ppermute | solution.py:43
  133.6 141.1 %collective-permute-start.14 = (bf16[5,1,2048]{2,1,0:T(2,128)(2,1)}, bf16[5,1,2048]{2,1,0:T(2,128)(2,1)}, u32[]{:S(2)}, u32[]{:S(2)}) collective-permute-start(bf16[5,1,2048]{2,1,0:T(2,128)(2,1)} %get-tuple-element.5), channel_id=1, source_target_pairs={{0,1},{1,2},{2,3},{4,5},{5,6},{6,7},{8,9},{9,10},{10,11},{12,13},{... | collective-permute-start | bytes 61448 | tf_op jit(solution)/shard_map/ppermute | solution.py:42
  144.9 26.5 %all-to-all-start.4 = ((bf16[3,64,1024]{2,0,1:T(4,128)(2,1)}), bf16[3,64,1024]{2,0,1:T(4,128)(2,1)}, u32[]{:S(2)}, u32[]{:S(2)}) async-start(bf16[3,64,1024]{2,0,1:T(4,128)(2,1)} %copy.156), calls=%async_computation.4 | async-start | bytes 1048576 | tf_op jit(solution)/shard_map/all_to_all | solution.py:176
  149.0 124.4 %reduce-scatter.5.cloned.1.call-start = ((), (), s32[]{:S(2)}) async-start(), calls=%async_computation.12 | async-start | bytes 3932160 | tf_op jit(solution)/shard_map/reduce_scatter | solution.py:165
  162.7 102.2 %collective-permute-start.2 = (bf16[5,1,2048]{2,1,0:T(2,128)(2,1)}, bf16[5,1,2048]{2,1,0:T(2,128)(2,1)}, u32[]{:S(2)}, u32[]{:S(2)}) collective-permute-start(bf16[5,1,2048]{2,1,0:T(2,128)(2,1)} %get-tuple-element.6), channel_id=1, source_target_pairs={{0,1},{1,2},{2,3},{4,5},{5,6},{6,7},{8,9},{9,10},{10,11},{12,13},{... | collective-permute-start | bytes 61448 | tf_op jit(solution)/shard_map/ppermute | solution.py:42
  164.6 100.3 %collective-permute-start.3 = (bf16[5,1,2048]{2,1,0:T(2,128)(2,1)}, bf16[5,1,2048]{2,1,0:T(2,128)(2,1)}, u32[]{:S(2)}, u32[]{:S(2)}) collective-permute-start(bf16[5,1,2048]{2,1,0:T(2,128)(2,1)} %get-tuple-element.7), channel_id=1, source_target_pairs={{1,0},{2,1},{3,2},{5,4},{6,5},{7,6},{9,8},{10,9},{11,10},{13,12},{... | collective-permute-start | bytes 61448 | tf_op jit(solution)/shard_map/ppermute | solution.py:43
  185.7 27.4 %all-to-all-start.6 = ((bf16[24,8,1024]{2,1,0:T(8,128)(2,1)}), bf16[24,8,1024]{2,1,0:T(8,128)(2,1)S(1)}, u32[]{:S(2)}, u32[]{:S(2)}) async-start(bf16[24,8,1024]{2,1,0:T(8,128)(2,1)} %convert_element_type.185), calls=%async_computation.7 | async-start | bytes 786432 | tf_op jit(solution)/shard_map/all_to_all | solution.py:200
  200.1 10.1 %collective-permute-start.4 = (bf16[3,8,1024]{2,1,0:T(8,128)(2,1)}, bf16[3,8,1024]{2,1,0:T(8,128)(2,1)}, u32[]{:S(2)}, u32[]{:S(2)}) collective-permute-start(bf16[3,8,1024]{2,1,0:T(8,128)(2,1)} %get-tuple-element.30), channel_id=1, source_target_pairs={{0,4},{4,0},{8,12},{12,8},{16,20},{20,16},{24,28},{28,24},{1,5},{5... | collective-permute-start | bytes 147464 | tf_op jit(solution)/shard_map/ppermute | solution.py:30
  210.2 7.0 %collective-permute-start.5 = (bf16[3,8,1024]{2,1,0:T(8,128)(2,1)}, bf16[3,8,1024]{2,1,0:T(8,128)(2,1)}, u32[]{:S(2)}, u32[]{:S(2)}) collective-permute-start(bf16[3,8,1024]{2,1,0:T(8,128)(2,1)} %get-tuple-element.29), channel_id=1, source_target_pairs={{0,8},{4,12},{8,0},{12,4},{16,24},{20,28},{24,16},{28,20},{1,9},{5... | collective-permute-start | bytes 147464 | tf_op jit(solution)/shard_map/ppermute | solution.py:30
  213.1 34.5 %all-to-all-start.5 = ((bf16[24,8,1024]{2,1,0:T(8,128)(2,1)}), bf16[24,8,1024]{2,1,0:T(8,128)(2,1)}, u32[]{:S(2)}, u32[]{:S(2)}) async-start(bf16[24,8,1024]{2,1,0:T(8,128)(2,1)} %convert_element_type.181), calls=%async_computation.5 | async-start | bytes 786432 | tf_op jit(solution)/shard_map/all_to_all | solution.py:199
  217.2 8.4 %collective-permute-start.6 = (bf16[3,8,1024]{2,1,0:T(8,128)(2,1)}, bf16[3,8,1024]{2,1,0:T(8,128)(2,1)S(1)}, u32[]{:S(2)}, u32[]{:S(2)}) collective-permute-start(bf16[3,8,1024]{2,1,0:T(8,128)(2,1)} %get-tuple-element.28), channel_id=1, source_target_pairs={{0,12},{4,8},{8,4},{12,0},{16,28},{20,24},{24,20},{28,16},{1,13},{... | collective-permute-start | bytes 147464 | tf_op jit(solution)/shard_map/ppermute | solution.py:30
  225.5 7.3 %collective-permute-start.7 = (bf16[3,8,1024]{2,1,0:T(8,128)(2,1)}, bf16[3,8,1024]{2,1,0:T(8,128)(2,1)S(1)}, u32[]{:S(2)}, u32[]{:S(2)}) collective-permute-start(bf16[3,8,1024]{2,1,0:T(8,128)(2,1)} %get-tuple-element.27), channel_id=1, source_target_pairs={{0,16},{4,20},{8,24},{12,28},{16,0},{20,4},{24,8},{28,12},{1,17},{... | collective-permute-start | bytes 147464 | tf_op jit(solution)/shard_map/ppermute | solution.py:30
  245.2 7.8 %collective-permute-start.10 = (bf16[3,8,1024]{2,1,0:T(8,128)(2,1)}, bf16[3,8,1024]{2,1,0:T(8,128)(2,1)}, u32[]{:S(2)}, u32[]{:S(2)}) collective-permute-start(bf16[3,8,1024]{2,1,0:T(8,128)(2,1)} %get-tuple-element.24), channel_id=1, source_target_pairs={{0,28},{4,24},{8,20},{12,16},{16,12},{20,8},{24,4},{28,0},{1,29},{... | collective-permute-start | bytes 147464 | tf_op jit(solution)/shard_map/ppermute | solution.py:30
  247.5 13.3 %all-to-all-start.3 = ((bf16[24,8,1024]{2,1,0:T(8,128)(2,1)}), bf16[24,8,1024]{2,1,0:T(8,128)(2,1)}, u32[]{:S(2)}, u32[]{:S(2)}) async-start(bf16[24,8,1024]{2,1,0:T(8,128)(2,1)} %convert_element_type.159), calls=%async_computation.3 | async-start | bytes 786432 | tf_op jit(solution)/shard_map/all_to_all | solution.py:198
  (31 other events, 206.5 us)
Sparse Core Ops, SparseCore 0:
  10.2 22.3 all-gather.2
  34.7 19.6 all-gather.4
  72.3 37.9 reduce-scatter.2
  159.5 38.3 reduce-scatter.4
